TPU v7x, 512 devices: a whole 4x4x16 slice. The times are simulated.
512 devices in a mesh: shard: 128 (over z, x, core), tensor: 4 (over y).
Axes of the slice: x: 4, y: 4, z: 16, core: 2. Of those that a mesh axis runs over, the one named last changes fastest.
Arguments:
- grads: bfloat16 [128, 4, 1536, 1024], P('shard', None, None, 'tensor'), may hold values from -240 to 240
- master: float32 [1536, 1024], P('shard', 'tensor'), may hold values from -3 to 3
- moment1: float32 [1536, 1024], P('shard', 'tensor'), may hold values from -3 to 3
- moment2: float32 [1536, 1024], P('shard', 'tensor'), may hold values from 0.25 to 1
- ema: float32 [1536, 1024], P('shard', 'tensor'), may hold values from -3 to 3
Outputs:
- new_master: float32 [1536, 1024], P('shard', 'tensor')
- new_moment1: float32 [1536, 1024], P('shard', 'tensor')
- new_moment2: float32 [1536, 1024], P('shard', 'tensor')
- new_ema: float32 [1536, 1024], P('shard', 'tensor')
- weights: bfloat16 [1536, 1024], P(None, 'tensor')
All inputs are finite; a program needn't handle non-finite values.
Results may differ from a plain program's by a relative error of at most 0.0004.
Values may be sent and summed in bfloat16 or wider, within the bound.
No kernel may reach another device: no remote copies, remote signals or barrier semaphores. Data moves between devices by JAX's collectives and lax.ppermute only.
A program may use at most 64 MiB of HBM per device.

v0:
```python
import jax
import jax.numpy as jnp
from jax import lax
from jax.sharding import PartitionSpec as P

STEP = 10
beta_one = 0.9
beta_two = 0.95
learn_rate = 0.02
decay_weight = 0.1
ema_keep = 0.99


def shards(grads, master, moment1, moment2, ema):
    local = grads[0]
    elements = local.shape[1] * local.shape[2] * lax.axis_size("tensor")
    summed = jnp.sum(local.astype(jnp.float32), axis=0)
    grad_part = lax.psum_scatter(summed, "shard", scatter_dimension=0, tiled=True)
    sq = lax.psum(jnp.sum(grad_part * grad_part), ("shard", "tensor"))
    scale = jnp.minimum(1.0, 1.0 / jnp.sqrt(sq / elements + 1e-06))
    clipped = scale * grad_part
    new_moment1 = beta_one * moment1 + (1.0 - beta_one) * clipped
    new_moment2 = beta_two * moment2 + (1.0 - beta_two) * clipped * clipped
    first_hat = new_moment1 / (1.0 - beta_one**STEP)
    second_hat = new_moment2 / (1.0 - beta_two**STEP)
    new_master = master - learn_rate * (
        first_hat / (jnp.sqrt(second_hat) + 1e-08) + decay_weight * master
    )
    new_ema = ema_keep * ema + (1.0 - ema_keep) * new_master
    weights = lax.all_gather(new_master.astype(jnp.bfloat16), "shard", axis=0, tiled=True)
    return (new_master, new_moment1, new_moment2, new_ema, weights)


def solution(mesh):
    return jax.shard_map(
        shards,
        mesh=mesh,
        in_specs=(
            P("shard", None, None, "tensor"),
            P("shard", "tensor"),
            P("shard", "tensor"),
            P("shard", "tensor"),
            P("shard", "tensor"),
        ),
        out_specs=(
            P("shard", "tensor"),
            P("shard", "tensor"),
            P("shard", "tensor"),
            P("shard", "tensor"),
            P(None, "tensor"),
        ),
        check_vma=False,
    )
```

profile of v0, /device:TPU:1, one launch (start us, length us, event | category | flops | bytes accessed | tf_op | source)
XLA Modules:
  0.0 570.4 jit_solution(2033311778829565577)
XLA Ops:
  0.6 2.5 convert_reduce_fusion
  3.1 0.0 copy-start.2
  3.1 0.0 copy-start.3
  3.1 0.0 copy-start.4
  3.2 262.6 %fusion = f32[16,256]{1,0:T(8,128)S(1)} fusion(f32[1536,256]{1,0:T(8,128)S(1)} %convert_reduce_fusion), kind=kCustom, calls=%all-reduce-scatter | all-reduce-scatter fusion | flops 524289 | bytes 1591296
  265.8 0.0 copy-start.1
  265.8 3.0 collective-permute-start
  268.9 2.6 collective-permute-start.31
  271.5 1.3 collective-permute-start.1
  272.8 1.3 collective-permute-start.10
  274.1 2.4 collective-permute-start.11
  276.5 0.0 collective-permute-done.31
  276.5 7.0 %collective-permute-start.12 = (f32[16,256]{1,0:T(8,128)S(1)}, f32[16,256]{1,0:T(8,128)S(1)}, u32[]{:S(2)}, u32[]{:S(2)}) collective-permute-start(f32[16,256]{1,0:T(8,128)S(1)} %fusion), channel_id=1, source_target_pairs={{0,52},{4,56},{8,60},{12,64},{16,68},{20,72},{24,76},{28,80},{32,8... | collective-permute-start | bytes 49160
  283.6 5.3 collective-permute-start.13
  288.9 0.0 collective-permute-done.1
  288.9 8.9 %collective-permute-start.14 = (f32[16,256]{1,0:T(8,128)S(1)}, f32[16,256]{1,0:T(8,128)S(1)}, u32[]{:S(2)}, u32[]{:S(2)}) collective-permute-start(f32[16,256]{1,0:T(8,128)S(1)} %fusion), channel_id=1, source_target_pairs={{0,60},{4,64},{8,68},{12,72},{16,76},{20,80},{24,84},{28,88},{32,9... | collective-permute-start | bytes 49160
  297.8 1.3 collective-permute-start.15
  299.1 6.5 %collective-permute-start.16 = (f32[16,256]{1,0:T(8,128)S(1)}, f32[16,256]{1,0:T(8,128)S(1)}, u32[]{:S(2)}, u32[]{:S(2)}) collective-permute-start(f32[16,256]{1,0:T(8,128)S(1)} %fusion), channel_id=1, source_target_pairs={{0,68},{4,72},{8,76},{12,80},{16,84},{20,88},{24,92},{28,96},{32,1... | collective-permute-start | bytes 49160
  305.6 2.8 collective-permute-start.17
  308.4 4.0 collective-permute-start.18
  312.4 2.9 collective-permute-start.19
  315.3 3.0 collective-permute-start.2
  318.3 1.4 collective-permute-start.20
  319.7 2.7 collective-permute-start.21
  322.4 1.3 collective-permute-start.22
  323.7 1.3 collective-permute-start.23
  325.0 1.8 collective-permute-start.24
  326.9 1.6 collective-permute-start.25
  328.5 3.2 collective-permute-start.26
  331.8 2.8 collective-permute-start.27
  334.7 1.9 collective-permute-start.28
  336.6 1.6 collective-permute-start.29
  338.2 2.6 collective-permute-start.3
  340.9 1.8 collective-permute-start.30
  342.7 4.5 collective-permute-start.4
  347.2 1.3 collective-permute-start.5
  348.5 2.2 collective-permute-start.6
  350.8 3.0 collective-permute-start.7
  353.8 3.7 collective-permute-start.8
  357.5 1.3 collective-permute-start.9
  358.8 1.3 dynamic-slice.4
  360.7 3.7 concatenate
  364.4 0.6 multiply_reduce_fusion
  365.0 102.4 %psum.7 = f32[]{:T(128)} all-reduce(f32[]{:T(128)} %multiply_reduce_fusion), channel_id=1, replica_groups=mesh['shard'=128,'tensor'=4] {'shard','tensor'}, use_global_device_ids=true, to_apply=%region_3.0 | all-reduce | flops 1 | bytes 8 | tf_op jit(solution)/shard_map/psum | solution.py:19
  468.1 0.6 convert_bitcast_fusion
  468.7 100.0 %all-gather = bf16[128,12,256]{2,1,0:T(8,128)(2,1)S(1)} all-gather(bf16[1,12,256]{2,1,0:T(8,128)(2,1)S(1)} %get-tuple-element.5), channel_id=1, replica_groups=mesh['shard'=128,'tensor'=4] {'shard'}, dimensions={0}, use_global_device_ids=true | all-gather | bytes 792576 | tf_op jit(solution)/shard_map/all_gather | solution.py:30
  568.7 1.1 reshape.12
  569.7 0.6 multiply_add_fusion
  (37 shorter events, 0.1 us)
Async XLA Ops:
  3.1 465.0 %copy-start.2 = (f32[12,256]{1,0:T(8,128)S(1)}, f32[12,256]{1,0:T(8,128)}, u32[]{:S(2)}) copy-start(f32[12,256]{1,0:T(8,128)} %param.6) | copy-start | bytes 36868
  3.1 464.9 %copy-start.3 = (f32[12,256]{1,0:T(8,128)S(1)}, f32[12,256]{1,0:T(8,128)}, u32[]{:S(2)}) copy-start(f32[12,256]{1,0:T(8,128)} %param.7) | copy-start | bytes 36868
  3.1 464.9 %copy-start.4 = (f32[12,256]{1,0:T(8,128)S(1)}, f32[12,256]{1,0:T(8,128)}, u32[]{:S(2)}) copy-start(f32[12,256]{1,0:T(8,128)} %param.8) | copy-start | bytes 36868
  265.8 303.9 %copy-start.1 = (f32[12,256]{1,0:T(8,128)S(1)}, f32[12,256]{1,0:T(8,128)}, u32[]{:S(2)}) copy-start(f32[12,256]{1,0:T(8,128)} %param.9) | copy-start | bytes 36868
  265.8 17.7 %collective-permute-start = (f32[16,256]{1,0:T(8,128)S(1)}, f32[16,256]{1,0:T(8,128)S(1)}, u32[]{:S(2)}, u32[]{:S(2)}) collective-permute-start(f32[16,256]{1,0:T(8,128)S(1)} %fusion), channel_id=1, source_target_pairs={{0,4},{4,8},{8,12},{12,16},{16,20},{20,24},{24,28},{28,32},{32,36}... | collective-permute-start | bytes 49160
  268.9 7.7 %collective-permute-start.31 = (f32[12,256]{1,0:T(8,128)S(1)}, f32[12,256]{1,0:T(8,128)S(1)}, u32[]{:S(2)}, u32[]{:S(2)}) collective-permute-start(f32[12,256]{1,0:T(8,128)S(1)} %slice), channel_id=1, source_target_pairs={{0,128},{4,132},{8,136},{12,140},{16,144},{20,148},{24,152},{28,15... | collective-permute-start | bytes 36872
  271.5 17.4 %collective-permute-start.1 = (f32[16,256]{1,0:T(8,128)S(1)}, f32[16,256]{1,0:T(8,128)S(1)}, u32[]{:S(2)}, u32[]{:S(2)}) collective-permute-start(f32[16,256]{1,0:T(8,128)S(1)} %fusion), channel_id=1, source_target_pairs={{0,8},{4,12},{8,16},{12,20},{16,24},{20,28},{24,32},{28,36},{32,40... | collective-permute-start | bytes 49160
  272.8 25.0 %collective-permute-start.10 = (f32[16,256]{1,0:T(8,128)S(1)}, f32[16,256]{1,0:T(8,128)S(1)}, u32[]{:S(2)}, u32[]{:S(2)}) collective-permute-start(f32[16,256]{1,0:T(8,128)S(1)} %fusion), channel_id=1, source_target_pairs={{0,44},{4,48},{8,52},{12,56},{16,60},{20,64},{24,68},{28,72},{32,7... | collective-permute-start | bytes 49160
  274.1 25.0 %collective-permute-start.11 = (f32[16,256]{1,0:T(8,128)S(1)}, f32[16,256]{1,0:T(8,128)S(1)}, u32[]{:S(2)}, u32[]{:S(2)}) collective-permute-start(f32[16,256]{1,0:T(8,128)S(1)} %fusion), channel_id=1, source_target_pairs={{0,48},{4,52},{8,56},{12,60},{16,64},{20,68},{24,72},{28,76},{32,8... | collective-permute-start | bytes 49160
  276.5 29.1 %collective-permute-start.12 = (f32[16,256]{1,0:T(8,128)S(1)}, f32[16,256]{1,0:T(8,128)S(1)}, u32[]{:S(2)}, u32[]{:S(2)}) collective-permute-start(f32[16,256]{1,0:T(8,128)S(1)} %fusion), channel_id=1, source_target_pairs={{0,52},{4,56},{8,60},{12,64},{16,68},{20,72},{24,76},{28,80},{32,8... | collective-permute-start | bytes 49160
  283.6 24.8 %collective-permute-start.13 = (f32[16,256]{1,0:T(8,128)S(1)}, f32[16,256]{1,0:T(8,128)S(1)}, u32[]{:S(2)}, u32[]{:S(2)}) collective-permute-start(f32[16,256]{1,0:T(8,128)S(1)} %fusion), channel_id=1, source_target_pairs={{0,56},{4,60},{8,64},{12,68},{16,72},{20,76},{24,80},{28,84},{32,8... | collective-permute-start | bytes 49160
  288.9 23.5 %collective-permute-start.14 = (f32[16,256]{1,0:T(8,128)S(1)}, f32[16,256]{1,0:T(8,128)S(1)}, u32[]{:S(2)}, u32[]{:S(2)}) collective-permute-start(f32[16,256]{1,0:T(8,128)S(1)} %fusion), channel_id=1, source_target_pairs={{0,60},{4,64},{8,68},{12,72},{16,76},{20,80},{24,84},{28,88},{32,9... | collective-permute-start | bytes 49160
  297.8 17.5 %collective-permute-start.15 = (f32[16,256]{1,0:T(8,128)S(1)}, f32[16,256]{1,0:T(8,128)S(1)}, u32[]{:S(2)}, u32[]{:S(2)}) collective-permute-start(f32[16,256]{1,0:T(8,128)S(1)} %fusion), channel_id=1, source_target_pairs={{0,64},{4,68},{8,72},{12,76},{16,80},{20,84},{24,88},{28,92},{32,9... | collective-permute-start | bytes 49160
  299.1 19.2 %collective-permute-start.16 = (f32[16,256]{1,0:T(8,128)S(1)}, f32[16,256]{1,0:T(8,128)S(1)}, u32[]{:S(2)}, u32[]{:S(2)}) collective-permute-start(f32[16,256]{1,0:T(8,128)S(1)} %fusion), channel_id=1, source_target_pairs={{0,68},{4,72},{8,76},{12,80},{16,84},{20,88},{24,92},{28,96},{32,1... | collective-permute-start | bytes 49160
  305.6 14.1 %collective-permute-start.17 = (f32[16,256]{1,0:T(8,128)S(1)}, f32[16,256]{1,0:T(8,128)S(1)}, u32[]{:S(2)}, u32[]{:S(2)}) collective-permute-start(f32[16,256]{1,0:T(8,128)S(1)} %fusion), channel_id=1, source_target_pairs={{0,72},{4,76},{8,80},{12,84},{16,88},{20,92},{24,96},{28,100},{32,... | collective-permute-start | bytes 49160
  308.4 14.0 %collective-permute-start.18 = (f32[16,256]{1,0:T(8,128)S(1)}, f32[16,256]{1,0:T(8,128)S(1)}, u32[]{:S(2)}, u32[]{:S(2)}) collective-permute-start(f32[16,256]{1,0:T(8,128)S(1)} %fusion), channel_id=1, source_target_pairs={{0,76},{4,80},{8,84},{12,88},{16,92},{20,96},{24,100},{28,104},{32... | collective-permute-start | bytes 49160
  312.4 11.3 %collective-permute-start.19 = (f32[16,256]{1,0:T(8,128)S(1)}, f32[16,256]{1,0:T(8,128)S(1)}, u32[]{:S(2)}, u32[]{:S(2)}) collective-permute-start(f32[16,256]{1,0:T(8,128)S(1)} %fusion), channel_id=1, source_target_pairs={{0,80},{4,84},{8,88},{12,92},{16,96},{20,100},{24,104},{28,108},{3... | collective-permute-start | bytes 49160
  315.3 9.8 %collective-permute-start.2 = (f32[16,256]{1,0:T(8,128)S(1)}, f32[16,256]{1,0:T(8,128)S(1)}, u32[]{:S(2)}, u32[]{:S(2)}) collective-permute-start(f32[16,256]{1,0:T(8,128)S(1)} %fusion), channel_id=1, source_target_pairs={{0,12},{4,16},{8,20},{12,24},{16,28},{20,32},{24,36},{28,40},{32,4... | collective-permute-start | bytes 49160
  318.3 8.5 %collective-permute-start.20 = (f32[16,256]{1,0:T(8,128)S(1)}, f32[16,256]{1,0:T(8,128)S(1)}, u32[]{:S(2)}, u32[]{:S(2)}) collective-permute-start(f32[16,256]{1,0:T(8,128)S(1)} %fusion), channel_id=1, source_target_pairs={{0,84},{4,88},{8,92},{12,96},{16,100},{20,104},{24,108},{28,112},{... | collective-permute-start | bytes 49160
  319.7 8.8 %collective-permute-start.21 = (f32[16,256]{1,0:T(8,128)S(1)}, f32[16,256]{1,0:T(8,128)S(1)}, u32[]{:S(2)}, u32[]{:S(2)}) collective-permute-start(f32[16,256]{1,0:T(8,128)S(1)} %fusion), channel_id=1, source_target_pairs={{0,88},{4,92},{8,96},{12,100},{16,104},{20,108},{24,112},{28,116},... | collective-permute-start | bytes 49160
  322.4 9.4 %collective-permute-start.22 = (f32[16,256]{1,0:T(8,128)S(1)}, f32[16,256]{1,0:T(8,128)S(1)}, u32[]{:S(2)}, u32[]{:S(2)}) collective-permute-start(f32[16,256]{1,0:T(8,128)S(1)} %fusion), channel_id=1, source_target_pairs={{0,92},{4,96},{8,100},{12,104},{16,108},{20,112},{24,116},{28,120}... | collective-permute-start | bytes 49160
  323.7 10.9 %collective-permute-start.23 = (f32[16,256]{1,0:T(8,128)S(1)}, f32[16,256]{1,0:T(8,128)S(1)}, u32[]{:S(2)}, u32[]{:S(2)}) collective-permute-start(f32[16,256]{1,0:T(8,128)S(1)} %fusion), channel_id=1, source_target_pairs={{0,96},{4,100},{8,104},{12,108},{16,112},{20,116},{24,120},{28,124... | collective-permute-start | bytes 49160
  325.0 11.5 %collective-permute-start.24 = (f32[16,256]{1,0:T(8,128)S(1)}, f32[16,256]{1,0:T(8,128)S(1)}, u32[]{:S(2)}, u32[]{:S(2)}) collective-permute-start(f32[16,256]{1,0:T(8,128)S(1)} %fusion), channel_id=1, source_target_pairs={{0,100},{4,104},{8,108},{12,112},{16,116},{20,120},{24,124},{28,12... | collective-permute-start | bytes 49160
  326.9 11.4 %collective-permute-start.25 = (f32[16,256]{1,0:T(8,128)S(1)}, f32[16,256]{1,0:T(8,128)S(1)}, u32[]{:S(2)}, u32[]{:S(2)}) collective-permute-start(f32[16,256]{1,0:T(8,128)S(1)} %fusion), channel_id=1, source_target_pairs={{0,104},{4,108},{8,112},{12,116},{16,120},{20,124},{24,128},{28,13... | collective-permute-start | bytes 49160
  328.5 12.3 %collective-permute-start.26 = (f32[16,256]{1,0:T(8,128)S(1)}, f32[16,256]{1,0:T(8,128)S(1)}, u32[]{:S(2)}, u32[]{:S(2)}) collective-permute-start(f32[16,256]{1,0:T(8,128)S(1)} %fusion), channel_id=1, source_target_pairs={{0,108},{4,112},{8,116},{12,120},{16,124},{20,128},{24,132},{28,13... | collective-permute-start | bytes 49160
  331.8 10.9 %collective-permute-start.27 = (f32[16,256]{1,0:T(8,128)S(1)}, f32[16,256]{1,0:T(8,128)S(1)}, u32[]{:S(2)}, u32[]{:S(2)}) collective-permute-start(f32[16,256]{1,0:T(8,128)S(1)} %fusion), channel_id=1, source_target_pairs={{0,112},{4,116},{8,120},{12,124},{16,128},{20,132},{24,136},{28,14... | collective-permute-start | bytes 49160
  334.7 12.6 %collective-permute-start.28 = (f32[16,256]{1,0:T(8,128)S(1)}, f32[16,256]{1,0:T(8,128)S(1)}, u32[]{:S(2)}, u32[]{:S(2)}) collective-permute-start(f32[16,256]{1,0:T(8,128)S(1)} %fusion), channel_id=1, source_target_pairs={{0,116},{4,120},{8,124},{12,128},{16,132},{20,136},{24,140},{28,14... | collective-permute-start | bytes 49160
  336.6 11.9 %collective-permute-start.29 = (f32[16,256]{1,0:T(8,128)S(1)}, f32[16,256]{1,0:T(8,128)S(1)}, u32[]{:S(2)}, u32[]{:S(2)}) collective-permute-start(f32[16,256]{1,0:T(8,128)S(1)} %fusion), channel_id=1, source_target_pairs={{0,120},{4,124},{8,128},{12,132},{16,136},{20,140},{24,144},{28,14... | collective-permute-start | bytes 49160
  338.2 12.5 %collective-permute-start.3 = (f32[16,256]{1,0:T(8,128)S(1)}, f32[16,256]{1,0:T(8,128)S(1)}, u32[]{:S(2)}, u32[]{:S(2)}) collective-permute-start(f32[16,256]{1,0:T(8,128)S(1)} %fusion), channel_id=1, source_target_pairs={{0,16},{4,20},{8,24},{12,28},{16,32},{20,36},{24,40},{28,44},{32,4... | collective-permute-start | bytes 49160
  340.9 12.9 %collective-permute-start.30 = (f32[16,256]{1,0:T(8,128)S(1)}, f32[16,256]{1,0:T(8,128)S(1)}, u32[]{:S(2)}, u32[]{:S(2)}) collective-permute-start(f32[16,256]{1,0:T(8,128)S(1)} %fusion), channel_id=1, source_target_pairs={{0,124},{4,128},{8,132},{12,136},{16,140},{20,144},{24,148},{28,15... | collective-permute-start | bytes 49160
  342.7 14.7 %collective-permute-start.4 = (f32[16,256]{1,0:T(8,128)S(1)}, f32[16,256]{1,0:T(8,128)S(1)}, u32[]{:S(2)}, u32[]{:S(2)}) collective-permute-start(f32[16,256]{1,0:T(8,128)S(1)} %fusion), channel_id=1, source_target_pairs={{0,20},{4,24},{8,28},{12,32},{16,36},{20,40},{24,44},{28,48},{32,5... | collective-permute-start | bytes 49160
  347.2 13.5 %collective-permute-start.5 = (f32[16,256]{1,0:T(8,128)S(1)}, f32[16,256]{1,0:T(8,128)S(1)}, u32[]{:S(2)}, u32[]{:S(2)}) collective-permute-start(f32[16,256]{1,0:T(8,128)S(1)} %fusion), channel_id=1, source_target_pairs={{0,24},{4,28},{8,32},{12,36},{16,40},{20,44},{24,48},{28,52},{32,5... | collective-permute-start | bytes 49160
  348.5 12.2 %collective-permute-start.6 = (f32[16,256]{1,0:T(8,128)S(1)}, f32[16,256]{1,0:T(8,128)S(1)}, u32[]{:S(2)}, u32[]{:S(2)}) collective-permute-start(f32[16,256]{1,0:T(8,128)S(1)} %fusion), channel_id=1, source_target_pairs={{0,28},{4,32},{8,36},{12,40},{16,44},{20,48},{24,52},{28,56},{32,6... | collective-permute-start | bytes 49160
  350.8 9.9 %collective-permute-start.7 = (f32[16,256]{1,0:T(8,128)S(1)}, f32[16,256]{1,0:T(8,128)S(1)}, u32[]{:S(2)}, u32[]{:S(2)}) collective-permute-start(f32[16,256]{1,0:T(8,128)S(1)} %fusion), channel_id=1, source_target_pairs={{0,32},{4,36},{8,40},{12,44},{16,48},{20,52},{24,56},{28,60},{32,6... | collective-permute-start | bytes 49160
  353.8 6.9 %collective-permute-start.8 = (f32[16,256]{1,0:T(8,128)S(1)}, f32[16,256]{1,0:T(8,128)S(1)}, u32[]{:S(2)}, u32[]{:S(2)}) collective-permute-start(f32[16,256]{1,0:T(8,128)S(1)} %fusion), channel_id=1, source_target_pairs={{0,36},{4,40},{8,44},{12,48},{16,52},{20,56},{24,60},{28,64},{32,6... | collective-permute-start | bytes 49160
  357.5 3.3 collective-permute-start.9
  468.7 101.6 %copy-start = (f32[12,256]{1,0:T(8,128)}, f32[12,256]{1,0:T(8,128)S(1)}, u32[]{:S(2)}) copy-start(f32[12,256]{1,0:T(8,128)S(1)} %get-tuple-element.6) | copy-start | bytes 36868
where the time goes:
time: 572 us; the launch traced here: 570 us
  blocking collectives  465 us (81%)
  starting transfers between devices  92.4 us (16%)
  local copies, waits for them, and re-layouts  6.01 us (1%)
    unnamed x1, blocking collectives  263 us
    psum x1, blocking collectives, shards(): sq = lax.psum(jnp.sum(grad_part * grad_part), ('shard', 'tensor'))  102 us
    all_gather x1, blocking collectives, shards(): lax.all_gather(new_master.astype(jnp.bfloat16), 'shard', axis=0, tiled=True)  100 us
    unnamed x32, starting transfers between devices  92.4 us
  transfers between devices with their start and end apart: 32, of which 0 were waited for; matrix products, arithmetic and copies ran while one was open for 0% of the time, Pallas kernels for 0%

commit v1 on v0

--- a/solution.py
+++ b/solution.py
@@ -27,7 +27,12 @@
         first_hat / (jnp.sqrt(second_hat) + 1e-08) + decay_weight * master
     )
     new_ema = ema_keep * ema + (1.0 - ema_keep) * new_master
-    weights = lax.all_gather(new_master.astype(jnp.bfloat16), "shard", axis=0, tiled=True)
+    weights = jnp.concatenate(
+        lax.all_to_all(
+            jnp.stack([new_master.astype(jnp.bfloat16)] * lax.axis_size("shard")), "shard", 0, 0
+        ),
+        axis=0,
+    )
     return (new_master, new_moment1, new_moment2, new_ema, weights)
 
 

time: 572 us -> 537 us (0.939)
  blocking collectives: 465 us -> 365 us
  waiting for transfers between devices: 0.08 us -> 51.3 us
  starting transfers between devices: 92.4 us -> 102 us
    all_gather x1 -> x0, blocking collectives: 100 us -> none  [shards(): lax.all_gather(new_master.astype(jnp.bfloat16), 'shard', axis=0, tiled=True)]
    all_to_all x0 -> x1, waiting for transfers between devices: none -> 51.2 us  [shards(): lax.all_to_all(jnp.stack([new_master.astype(jnp.bfloat16)] * lax.axis_siz...]
    all_to_all x0 -> x1, starting transfers between devices: none -> 9.92 us  [shards(): lax.all_to_all(jnp.stack([new_master.astype(jnp.bfloat16)] * lax.axis_siz...]
  transfers between devices with their start and end apart: 32 -> 33, of which waited for: 0 -> 1; matrix products, arithmetic and copies ran while one was open for 0% -> 0% of each run, Pallas kernels for 0% -> 0%
where the time goes in v1:
time: 537 us; the launch traced here: 533 us
  blocking collectives  365 us (68%)
  starting transfers between devices  102 us (19%)
  waiting for transfers between devices  51.3 us (10%)
  local copies, waits for them, and re-layouts  7.09 us (1%)
    unnamed x1, blocking collectives  263 us
    psum x1, blocking collectives, shards(): sq = lax.psum(jnp.sum(grad_part * grad_part), ('shard', 'tensor'))  102 us
    unnamed x32, starting transfers between devices  92.4 us
    all_to_all x1, waiting for transfers between devices, shards(): lax.all_to_all(jnp.stack([new_master.astype(jnp.bfloat16)] * lax.axis_siz...  51.2 us
  transfers between devices with their start and end apart: 33, of which 1 were waited for; matrix products, arithmetic and copies ran while one was open for 0% of the time, Pallas kernels for 0%

profile of v1, /device:TPU:1, one launch (start us, length us, event | category | flops | bytes accessed | tf_op | source)
XLA Modules:
  0.0 532.6 jit_solution(195749372045197919)
XLA Ops:
  0.6 2.5 convert_reduce_fusion
  3.1 0.0 copy-start.2
  3.1 0.0 copy-start.3
  3.1 0.0 copy-start.4
  3.2 262.6 %fusion = f32[16,256]{1,0:T(8,128)S(1)} fusion(f32[1536,256]{1,0:T(8,128)S(1)} %convert_reduce_fusion), kind=kCustom, calls=%all-reduce-scatter | all-reduce-scatter fusion | flops 524289 | bytes 1591296
  265.8 3.0 collective-permute-start
  268.8 2.6 collective-permute-start.31
  271.5 1.3 collective-permute-start.1
  272.8 1.3 collective-permute-start.10
  274.1 2.4 collective-permute-start.11
  276.5 7.0 %collective-permute-start.12 = (f32[16,256]{1,0:T(8,128)S(1)}, f32[16,256]{1,0:T(8,128)S(1)}, u32[]{:S(2)}, u32[]{:S(2)}) collective-permute-start(f32[16,256]{1,0:T(8,128)S(1)} %fusion), channel_id=1, source_target_pairs={{0,52},{4,56},{8,60},{12,64},{16,68},{20,72},{24,76},{28,80},{32,8... | collective-permute-start | bytes 49160
  283.6 5.3 collective-permute-start.13
  288.9 8.9 %collective-permute-start.14 = (f32[16,256]{1,0:T(8,128)S(1)}, f32[16,256]{1,0:T(8,128)S(1)}, u32[]{:S(2)}, u32[]{:S(2)}) collective-permute-start(f32[16,256]{1,0:T(8,128)S(1)} %fusion), channel_id=1, source_target_pairs={{0,60},{4,64},{8,68},{12,72},{16,76},{20,80},{24,84},{28,88},{32,9... | collective-permute-start | bytes 49160
  297.8 1.3 collective-permute-start.15
  299.1 6.5 %collective-permute-start.16 = (f32[16,256]{1,0:T(8,128)S(1)}, f32[16,256]{1,0:T(8,128)S(1)}, u32[]{:S(2)}, u32[]{:S(2)}) collective-permute-start(f32[16,256]{1,0:T(8,128)S(1)} %fusion), channel_id=1, source_target_pairs={{0,68},{4,72},{8,76},{12,80},{16,84},{20,88},{24,92},{28,96},{32,1... | collective-permute-start | bytes 49160
  305.6 2.8 collective-permute-start.17
  308.4 4.0 collective-permute-start.18
  312.4 2.9 collective-permute-start.19
  315.3 3.0 collective-permute-start.2
  318.3 1.4 collective-permute-start.20
  319.7 2.7 collective-permute-start.21
  322.4 1.3 collective-permute-start.22
  323.7 1.3 collective-permute-start.23
  325.0 1.8 collective-permute-start.24
  326.9 1.6 collective-permute-start.25
  328.5 3.2 collective-permute-start.26
  331.8 2.8 collective-permute-start.27
  334.7 1.9 collective-permute-start.28
  336.6 1.6 collective-permute-start.29
  338.2 2.6 collective-permute-start.3
  340.9 1.8 collective-permute-start.30
  342.7 4.5 collective-permute-start.4
  347.2 1.3 collective-permute-start.5
  348.5 2.2 collective-permute-start.6
  350.8 3.0 collective-permute-start.7
  353.8 3.7 collective-permute-start.8
  357.4 1.3 collective-permute-start.9
  358.7 1.3 dynamic-slice.4
  360.7 0.0 copy-start.1
  360.7 3.7 concatenate
  364.4 0.6 multiply_reduce_fusion
  365.0 102.4 %psum.7 = f32[]{:T(128)} all-reduce(f32[]{:T(128)} %multiply_reduce_fusion), channel_id=1, replica_groups=mesh['shard'=128,'tensor'=4] {'shard','tensor'}, use_global_device_ids=true, to_apply=%region_3.0 | all-reduce | flops 1 | bytes 8 | tf_op jit(solution)/shard_map/psum | solution.py:19
  468.1 0.6 fusion.2
  468.7 1.1 stack.2
  469.8 9.9 %all-to-all-start = ((bf16[128,12,256]{2,1,0:T(8,128)(2,1)}), bf16[128,12,256]{2,1,0:T(8,128)(2,1)S(1)}, u32[]{:S(2)}, u32[]{:S(2)}) async-start(bf16[128,12,256]{2,1,0:T(8,128)(2,1)} %stack.2), calls=%async_computation | async-start | bytes 2097152 | tf_op jit(solution)/shard_map/all_to_all | solution.py:31
  479.7 0.6 multiply_add_fusion
  480.4 51.2 %all-to-all-done = bf16[128,12,256]{2,1,0:T(8,128)(2,1)S(1)} async-done(((bf16[128,12,256]{2,1,0:T(8,128)(2,1)}), bf16[128,12,256]{2,1,0:T(8,128)(2,1)S(1)}, u32[]{:S(2)}, u32[]{:S(2)}) %all-to-all-start) | async-done | bytes 786464 | tf_op jit(solution)/shard_map/all_to_all | solution.py:31
  531.6 1.1 reshape.16
  (39 shorter events, 0.1 us)
Async XLA Ops:
  3.1 465.0 %copy-start.2 = (f32[12,256]{1,0:T(8,128)S(1)}, f32[12,256]{1,0:T(8,128)}, u32[]{:S(2)}) copy-start(f32[12,256]{1,0:T(8,128)} %param.6) | copy-start | bytes 36868
  3.1 464.9 %copy-start.3 = (f32[12,256]{1,0:T(8,128)S(1)}, f32[12,256]{1,0:T(8,128)}, u32[]{:S(2)}) copy-start(f32[12,256]{1,0:T(8,128)} %param.7) | copy-start | bytes 36868
  3.1 464.9 %copy-start.4 = (f32[12,256]{1,0:T(8,128)S(1)}, f32[12,256]{1,0:T(8,128)}, u32[]{:S(2)}) copy-start(f32[12,256]{1,0:T(8,128)} %param.8) | copy-start | bytes 36868
  265.8 17.7 %collective-permute-start = (f32[16,256]{1,0:T(8,128)S(1)}, f32[16,256]{1,0:T(8,128)S(1)}, u32[]{:S(2)}, u32[]{:S(2)}) collective-permute-start(f32[16,256]{1,0:T(8,128)S(1)} %fusion), channel_id=1, source_target_pairs={{0,4},{4,8},{8,12},{12,16},{16,20},{20,24},{24,28},{28,32},{32,36}... | collective-permute-start | bytes 49160
  268.8 7.7 %collective-permute-start.31 = (f32[12,256]{1,0:T(8,128)S(1)}, f32[12,256]{1,0:T(8,128)S(1)}, u32[]{:S(2)}, u32[]{:S(2)}) collective-permute-start(f32[12,256]{1,0:T(8,128)S(1)} %slice), channel_id=1, source_target_pairs={{0,128},{4,132},{8,136},{12,140},{16,144},{20,148},{24,152},{28,15... | collective-permute-start | bytes 36872
  271.5 17.4 %collective-permute-start.1 = (f32[16,256]{1,0:T(8,128)S(1)}, f32[16,256]{1,0:T(8,128)S(1)}, u32[]{:S(2)}, u32[]{:S(2)}) collective-permute-start(f32[16,256]{1,0:T(8,128)S(1)} %fusion), channel_id=1, source_target_pairs={{0,8},{4,12},{8,16},{12,20},{16,24},{20,28},{24,32},{28,36},{32,40... | collective-permute-start | bytes 49160
  272.8 25.0 %collective-permute-start.10 = (f32[16,256]{1,0:T(8,128)S(1)}, f32[16,256]{1,0:T(8,128)S(1)}, u32[]{:S(2)}, u32[]{:S(2)}) collective-permute-start(f32[16,256]{1,0:T(8,128)S(1)} %fusion), channel_id=1, source_target_pairs={{0,44},{4,48},{8,52},{12,56},{16,60},{20,64},{24,68},{28,72},{32,7... | collective-permute-start | bytes 49160
  274.1 25.0 %collective-permute-start.11 = (f32[16,256]{1,0:T(8,128)S(1)}, f32[16,256]{1,0:T(8,128)S(1)}, u32[]{:S(2)}, u32[]{:S(2)}) collective-permute-start(f32[16,256]{1,0:T(8,128)S(1)} %fusion), channel_id=1, source_target_pairs={{0,48},{4,52},{8,56},{12,60},{16,64},{20,68},{24,72},{28,76},{32,8... | collective-permute-start | bytes 49160
  276.5 29.1 %collective-permute-start.12 = (f32[16,256]{1,0:T(8,128)S(1)}, f32[16,256]{1,0:T(8,128)S(1)}, u32[]{:S(2)}, u32[]{:S(2)}) collective-permute-start(f32[16,256]{1,0:T(8,128)S(1)} %fusion), channel_id=1, source_target_pairs={{0,52},{4,56},{8,60},{12,64},{16,68},{20,72},{24,76},{28,80},{32,8... | collective-permute-start | bytes 49160
  283.6 24.8 %collective-permute-start.13 = (f32[16,256]{1,0:T(8,128)S(1)}, f32[16,256]{1,0:T(8,128)S(1)}, u32[]{:S(2)}, u32[]{:S(2)}) collective-permute-start(f32[16,256]{1,0:T(8,128)S(1)} %fusion), channel_id=1, source_target_pairs={{0,56},{4,60},{8,64},{12,68},{16,72},{20,76},{24,80},{28,84},{32,8... | collective-permute-start | bytes 49160
  288.9 23.5 %collective-permute-start.14 = (f32[16,256]{1,0:T(8,128)S(1)}, f32[16,256]{1,0:T(8,128)S(1)}, u32[]{:S(2)}, u32[]{:S(2)}) collective-permute-start(f32[16,256]{1,0:T(8,128)S(1)} %fusion), channel_id=1, source_target_pairs={{0,60},{4,64},{8,68},{12,72},{16,76},{20,80},{24,84},{28,88},{32,9... | collective-permute-start | bytes 49160
  297.8 17.5 %collective-permute-start.15 = (f32[16,256]{1,0:T(8,128)S(1)}, f32[16,256]{1,0:T(8,128)S(1)}, u32[]{:S(2)}, u32[]{:S(2)}) collective-permute-start(f32[16,256]{1,0:T(8,128)S(1)} %fusion), channel_id=1, source_target_pairs={{0,64},{4,68},{8,72},{12,76},{16,80},{20,84},{24,88},{28,92},{32,9... | collective-permute-start | bytes 49160
  299.1 19.2 %collective-permute-start.16 = (f32[16,256]{1,0:T(8,128)S(1)}, f32[16,256]{1,0:T(8,128)S(1)}, u32[]{:S(2)}, u32[]{:S(2)}) collective-permute-start(f32[16,256]{1,0:T(8,128)S(1)} %fusion), channel_id=1, source_target_pairs={{0,68},{4,72},{8,76},{12,80},{16,84},{20,88},{24,92},{28,96},{32,1... | collective-permute-start | bytes 49160
  305.6 14.1 %collective-permute-start.17 = (f32[16,256]{1,0:T(8,128)S(1)}, f32[16,256]{1,0:T(8,128)S(1)}, u32[]{:S(2)}, u32[]{:S(2)}) collective-permute-start(f32[16,256]{1,0:T(8,128)S(1)} %fusion), channel_id=1, source_target_pairs={{0,72},{4,76},{8,80},{12,84},{16,88},{20,92},{24,96},{28,100},{32,... | collective-permute-start | bytes 49160
  308.4 14.0 %collective-permute-start.18 = (f32[16,256]{1,0:T(8,128)S(1)}, f32[16,256]{1,0:T(8,128)S(1)}, u32[]{:S(2)}, u32[]{:S(2)}) collective-permute-start(f32[16,256]{1,0:T(8,128)S(1)} %fusion), channel_id=1, source_target_pairs={{0,76},{4,80},{8,84},{12,88},{16,92},{20,96},{24,100},{28,104},{32... | collective-permute-start | bytes 49160
  312.4 11.3 %collective-permute-start.19 = (f32[16,256]{1,0:T(8,128)S(1)}, f32[16,256]{1,0:T(8,128)S(1)}, u32[]{:S(2)}, u32[]{:S(2)}) collective-permute-start(f32[16,256]{1,0:T(8,128)S(1)} %fusion), channel_id=1, source_target_pairs={{0,80},{4,84},{8,88},{12,92},{16,96},{20,100},{24,104},{28,108},{3... | collective-permute-start | bytes 49160
  315.3 9.8 %collective-permute-start.2 = (f32[16,256]{1,0:T(8,128)S(1)}, f32[16,256]{1,0:T(8,128)S(1)}, u32[]{:S(2)}, u32[]{:S(2)}) collective-permute-start(f32[16,256]{1,0:T(8,128)S(1)} %fusion), channel_id=1, source_target_pairs={{0,12},{4,16},{8,20},{12,24},{16,28},{20,32},{24,36},{28,40},{32,4... | collective-permute-start | bytes 49160
  318.3 8.5 %collective-permute-start.20 = (f32[16,256]{1,0:T(8,128)S(1)}, f32[16,256]{1,0:T(8,128)S(1)}, u32[]{:S(2)}, u32[]{:S(2)}) collective-permute-start(f32[16,256]{1,0:T(8,128)S(1)} %fusion), channel_id=1, source_target_pairs={{0,84},{4,88},{8,92},{12,96},{16,100},{20,104},{24,108},{28,112},{... | collective-permute-start | bytes 49160
  319.7 8.8 %collective-permute-start.21 = (f32[16,256]{1,0:T(8,128)S(1)}, f32[16,256]{1,0:T(8,128)S(1)}, u32[]{:S(2)}, u32[]{:S(2)}) collective-permute-start(f32[16,256]{1,0:T(8,128)S(1)} %fusion), channel_id=1, source_target_pairs={{0,88},{4,92},{8,96},{12,100},{16,104},{20,108},{24,112},{28,116},... | collective-permute-start | bytes 49160
  322.4 9.4 %collective-permute-start.22 = (f32[16,256]{1,0:T(8,128)S(1)}, f32[16,256]{1,0:T(8,128)S(1)}, u32[]{:S(2)}, u32[]{:S(2)}) collective-permute-start(f32[16,256]{1,0:T(8,128)S(1)} %fusion), channel_id=1, source_target_pairs={{0,92},{4,96},{8,100},{12,104},{16,108},{20,112},{24,116},{28,120}... | collective-permute-start | bytes 49160
  323.7 10.9 %collective-permute-start.23 = (f32[16,256]{1,0:T(8,128)S(1)}, f32[16,256]{1,0:T(8,128)S(1)}, u32[]{:S(2)}, u32[]{:S(2)}) collective-permute-start(f32[16,256]{1,0:T(8,128)S(1)} %fusion), channel_id=1, source_target_pairs={{0,96},{4,100},{8,104},{12,108},{16,112},{20,116},{24,120},{28,124... | collective-permute-start | bytes 49160
  325.0 11.5 %collective-permute-start.24 = (f32[16,256]{1,0:T(8,128)S(1)}, f32[16,256]{1,0:T(8,128)S(1)}, u32[]{:S(2)}, u32[]{:S(2)}) collective-permute-start(f32[16,256]{1,0:T(8,128)S(1)} %fusion), channel_id=1, source_target_pairs={{0,100},{4,104},{8,108},{12,112},{16,116},{20,120},{24,124},{28,12... | collective-permute-start | bytes 49160
  326.9 11.4 %collective-permute-start.25 = (f32[16,256]{1,0:T(8,128)S(1)}, f32[16,256]{1,0:T(8,128)S(1)}, u32[]{:S(2)}, u32[]{:S(2)}) collective-permute-start(f32[16,256]{1,0:T(8,128)S(1)} %fusion), channel_id=1, source_target_pairs={{0,104},{4,108},{8,112},{12,116},{16,120},{20,124},{24,128},{28,13... | collective-permute-start | bytes 49160
  328.5 12.3 %collective-permute-start.26 = (f32[16,256]{1,0:T(8,128)S(1)}, f32[16,256]{1,0:T(8,128)S(1)}, u32[]{:S(2)}, u32[]{:S(2)}) collective-permute-start(f32[16,256]{1,0:T(8,128)S(1)} %fusion), channel_id=1, source_target_pairs={{0,108},{4,112},{8,116},{12,120},{16,124},{20,128},{24,132},{28,13... | collective-permute-start | bytes 49160
  331.8 10.9 %collective-permute-start.27 = (f32[16,256]{1,0:T(8,128)S(1)}, f32[16,256]{1,0:T(8,128)S(1)}, u32[]{:S(2)}, u32[]{:S(2)}) collective-permute-start(f32[16,256]{1,0:T(8,128)S(1)} %fusion), channel_id=1, source_target_pairs={{0,112},{4,116},{8,120},{12,124},{16,128},{20,132},{24,136},{28,14... | collective-permute-start | bytes 49160
  334.7 12.6 %collective-permute-start.28 = (f32[16,256]{1,0:T(8,128)S(1)}, f32[16,256]{1,0:T(8,128)S(1)}, u32[]{:S(2)}, u32[]{:S(2)}) collective-permute-start(f32[16,256]{1,0:T(8,128)S(1)} %fusion), channel_id=1, source_target_pairs={{0,116},{4,120},{8,124},{12,128},{16,132},{20,136},{24,140},{28,14... | collective-permute-start | bytes 49160
  336.6 11.9 %collective-permute-start.29 = (f32[16,256]{1,0:T(8,128)S(1)}, f32[16,256]{1,0:T(8,128)S(1)}, u32[]{:S(2)}, u32[]{:S(2)}) collective-permute-start(f32[16,256]{1,0:T(8,128)S(1)} %fusion), channel_id=1, source_target_pairs={{0,120},{4,124},{8,128},{12,132},{16,136},{20,140},{24,144},{28,14... | collective-permute-start | bytes 49160
  338.2 12.5 %collective-permute-start.3 = (f32[16,256]{1,0:T(8,128)S(1)}, f32[16,256]{1,0:T(8,128)S(1)}, u32[]{:S(2)}, u32[]{:S(2)}) collective-permute-start(f32[16,256]{1,0:T(8,128)S(1)} %fusion), channel_id=1, source_target_pairs={{0,16},{4,20},{8,24},{12,28},{16,32},{20,36},{24,40},{28,44},{32,4... | collective-permute-start | bytes 49160
  340.9 12.9 %collective-permute-start.30 = (f32[16,256]{1,0:T(8,128)S(1)}, f32[16,256]{1,0:T(8,128)S(1)}, u32[]{:S(2)}, u32[]{:S(2)}) collective-permute-start(f32[16,256]{1,0:T(8,128)S(1)} %fusion), channel_id=1, source_target_pairs={{0,124},{4,128},{8,132},{12,136},{16,140},{20,144},{24,148},{28,15... | collective-permute-start | bytes 49160
  342.7 14.7 %collective-permute-start.4 = (f32[16,256]{1,0:T(8,128)S(1)}, f32[16,256]{1,0:T(8,128)S(1)}, u32[]{:S(2)}, u32[]{:S(2)}) collective-permute-start(f32[16,256]{1,0:T(8,128)S(1)} %fusion), channel_id=1, source_target_pairs={{0,20},{4,24},{8,28},{12,32},{16,36},{20,40},{24,44},{28,48},{32,5... | collective-permute-start | bytes 49160
  347.2 13.5 %collective-permute-start.5 = (f32[16,256]{1,0:T(8,128)S(1)}, f32[16,256]{1,0:T(8,128)S(1)}, u32[]{:S(2)}, u32[]{:S(2)}) collective-permute-start(f32[16,256]{1,0:T(8,128)S(1)} %fusion), channel_id=1, source_target_pairs={{0,24},{4,28},{8,32},{12,36},{16,40},{20,44},{24,48},{28,52},{32,5... | collective-permute-start | bytes 49160
  348.5 12.2 %collective-permute-start.6 = (f32[16,256]{1,0:T(8,128)S(1)}, f32[16,256]{1,0:T(8,128)S(1)}, u32[]{:S(2)}, u32[]{:S(2)}) collective-permute-start(f32[16,256]{1,0:T(8,128)S(1)} %fusion), channel_id=1, source_target_pairs={{0,28},{4,32},{8,36},{12,40},{16,44},{20,48},{24,52},{28,56},{32,6... | collective-permute-start | bytes 49160
  350.8 9.9 %collective-permute-start.7 = (f32[16,256]{1,0:T(8,128)S(1)}, f32[16,256]{1,0:T(8,128)S(1)}, u32[]{:S(2)}, u32[]{:S(2)}) collective-permute-start(f32[16,256]{1,0:T(8,128)S(1)} %fusion), channel_id=1, source_target_pairs={{0,32},{4,36},{8,40},{12,44},{16,48},{20,52},{24,56},{28,60},{32,6... | collective-permute-start | bytes 49160
  353.8 6.9 %collective-permute-start.8 = (f32[16,256]{1,0:T(8,128)S(1)}, f32[16,256]{1,0:T(8,128)S(1)}, u32[]{:S(2)}, u32[]{:S(2)}) collective-permute-start(f32[16,256]{1,0:T(8,128)S(1)} %fusion), channel_id=1, source_target_pairs={{0,36},{4,40},{8,44},{12,48},{16,52},{20,56},{24,60},{28,64},{32,6... | collective-permute-start | bytes 49160
  357.4 3.3 collective-permute-start.9
  360.7 119.1 %copy-start.1 = (f32[12,256]{1,0:T(8,128)S(1)}, f32[12,256]{1,0:T(8,128)}, u32[]{:S(2)}) copy-start(f32[12,256]{1,0:T(8,128)} %param.9) | copy-start | bytes 36868
  468.7 63.9 %copy-start = (f32[12,256]{1,0:T(8,128)}, f32[12,256]{1,0:T(8,128)S(1)}, u32[]{:S(2)}) copy-start(f32[12,256]{1,0:T(8,128)S(1)} %get-tuple-element.6) | copy-start | bytes 36868
  469.8 61.8 %all-to-all-start = ((bf16[128,12,256]{2,1,0:T(8,128)(2,1)}), bf16[128,12,256]{2,1,0:T(8,128)(2,1)S(1)}, u32[]{:S(2)}, u32[]{:S(2)}) async-start(bf16[128,12,256]{2,1,0:T(8,128)(2,1)} %stack.2), calls=%async_computation | async-start | bytes 2097152 | tf_op jit(solution)/shard_map/all_to_all | solution.py:31
